TPU v7x, 32 devices: a whole 2x2x4 slice. The times are simulated.
32 devices in a mesh: line: 8 (over z, x), span: 4 (over y, core).
Axes of the slice: x: 2, y: 2, z: 4, core: 2. Of those that a mesh axis runs over, the one named last changes fastest.
Arguments:
- forcing: float32 [32, 256, 256], P('span', 'line'), may hold values from -1 to 1
- blocks: float32 [256, 256, 256], P(('line', 'span')), may hold values from -1 to 1
- upstream: float32 [256, 256], P(('line', 'span')), may hold values from -2 to 0
Outputs:
- solution: float32 [32, 256, 256], P('span', 'line')
All inputs are finite; a program needn't handle non-finite values.
Results may differ from a plain program's by a relative error of at most 0.0003.
Values sent between devices are 32-bit elements; how exact they have to be, the bound alone decides.
A program may use at most 192 MiB of HBM per device.

v0:
```python
import jax
import jax.numpy as jnp
from jax import lax
from jax.sharding import PartitionSpec as P


def carried_in(value, axis, join, neutral):
    count, mine = (lax.axis_size(axis), lax.axis_index(axis))
    pieces = jax.tree.map(lambda part: lax.all_gather(part, axis), value)
    running = jax.tree.map(
        lambda part, zero: jnp.full_like(part, 0) + jnp.asarray(zero, part.dtype), value, neutral
    )

    def turn(position, running):
        longer = join(running, jax.tree.map(lambda part: part[position], pieces))
        return jax.tree.map(lambda new, old: jnp.where(position < mine, new, old), longer, running)

    return lax.fori_loop(0, count - 1, turn, running)


def sweep(initial, cell_forcing, cell_blocks, cell_upstream):
    carried = initial
    pieces = []
    for cell in range(cell_blocks.shape[0]):
        carried = jnp.dot(
            cell_forcing[:, cell, :] - cell_upstream[cell][None, :] * carried,
            cell_blocks[cell],
            precision=lax.Precision.HIGHEST,
            preferred_element_type=jnp.float32,
        )
        pieces.append(carried)
    return jnp.stack(pieces, axis=1)


def spike_product(cell_blocks, cell_upstream):
    transfer = -cell_upstream[:, :, None] * cell_blocks
    product = transfer[0]
    for cell in range(1, cell_blocks.shape[0]):
        product = jnp.dot(
            product,
            transfer[cell],
            precision=lax.Precision.HIGHEST,
            preferred_element_type=jnp.float32,
        )
    return product


def combine(earlier, later):
    early_map, early_state = earlier
    late_map, late_state = later
    joined_map = jnp.dot(
        early_map, late_map, precision=lax.Precision.HIGHEST, preferred_element_type=jnp.float32
    )
    joined_state = (
        jnp.dot(
            early_state,
            late_map,
            precision=lax.Precision.HIGHEST,
            preferred_element_type=jnp.float32,
        )
        + late_state
    )
    return (joined_map, joined_state)


def shards(forcing, blocks, upstream):
    levels = blocks.shape[-1]
    identity_block = jnp.eye(levels, dtype=jnp.float32)
    local_forcing = lax.all_to_all(forcing, "span", split_axis=1, concat_axis=0, tiled=True)
    cell_blocks, cell_upstream = (blocks, upstream)
    zero_state = jnp.zeros((local_forcing.shape[0], levels), jnp.float32)
    trial = sweep(zero_state, local_forcing, cell_blocks, cell_upstream)
    last_states = trial[:, -1, :]
    spike_map = spike_product(cell_blocks, cell_upstream)
    span_count = lax.axis_size("span")
    group_maps, group_states = (
        lax.all_gather(spike_map[None], "span", axis=0, tiled=True),
        lax.all_gather(last_states[None], "span", axis=0, tiled=True),
    )
    prefix_maps = [identity_block]
    prefix_states = [zero_state]
    running = (group_maps[0], group_states[0])
    for member in range(1, span_count):
        prefix_maps.append(running[0])
        prefix_states.append(running[1])
        running = combine(running, (group_maps[member], group_states[member]))
    position = lax.axis_index("span")
    own_map = jnp.stack(prefix_maps)[position]
    own_state = jnp.stack(prefix_states)[position]
    group_prefix = carried_in(running, "line", combine, (identity_block, zero_state))
    incoming = combine(group_prefix, (own_map, own_state))[1]
    solved = sweep(incoming, local_forcing, cell_blocks, cell_upstream)
    return lax.all_to_all(solved, "span", split_axis=0, concat_axis=1, tiled=True)


def solution(mesh):
    placed = (P("span", "line", None), P(("line", "span"), None, None), P(("line", "span"), None))
    return jax.shard_map(
        shards, mesh=mesh, in_specs=placed, out_specs=P("span", "line", None), check_vma=False
    )
```

profile of v0, /device:TPU:0, one launch (start us, length us, event | category | flops | bytes accessed | tf_op | source)
XLA Modules:
  0.0 117.7 jit_solution(12809926064599229678)
XLA Ops:
  6.5 0.7 neg.4
  7.2 1.9 %broadcast_multiply_fusion = f32[8,256,256]{2,1,0:T(8,128)S(1)} fusion(f32[8,256,256]{2,1,0:T(8,128)} %param.6, f32[8,256]{1,0:T(8,128)S(1)} %neg.4), kind=kLoop, calls=%fused_computation.36 | loop fusion | flops 524288 | bytes 4202496 | tf_op jit(solution)/shard_map/mul | solution.py:36
  9.6 0.4 fusion.29
  10.0 0.4 fusion.28
  10.3 0.4 fusion.27
  10.7 0.4 fusion.26
  11.5 1.1 fusion.24
  12.6 0.9 copy.6
  13.5 4.4 %all-to-all-start = ((f32[8,32,256]{2,0,1:T(8,128)}), f32[8,32,256]{2,0,1:T(8,128)}, u32[]{:S(2)}, u32[]{:S(2)}) async-start(f32[8,32,256]{2,0,1:T(8,128)} %copy.6), calls=%async_computation | async-start | bytes 524288 | tf_op jit(solution)/shard_map/all_to_all | solution.py:69
  17.9 14.3 %all-gather.7.cloned.1.call-done = f32[1024,256]{1,0:T(8,128)} async-done(((f32[256,256]{1,0:T(8,128)}), f32[1024,256]{1,0:T(8,128)}) %all-gather.7.cloned.1.call-update) | async-done | bytes 1048592 | tf_op jit(solution)/shard_map/all_gather | solution.py:77
  32.2 1.4 %fusion.62 = f32[256,256]{1,0:T(8,128)S(1)} fusion(f32[1024,256]{1,0:T(8,128)} %all-gather.7.cloned.1.call-done), kind=kOutput, calls=%fused_computation.90 | convolution fusion | flops 201326592 | bytes 786432 | tf_op jit(solution)/shard_map/dot_general | solution.py:51
  33.6 1.3 %fusion.59 = f32[256,256]{1,0:T(8,128)S(1)} fusion(f32[256,256]{1,0:T(8,128)S(1)} %fusion.62, f32[1024,256]{1,0:T(8,128)} %all-gather.7.cloned.1.call-done), kind=kOutput, calls=%fused_computation.87 | convolution fusion | flops 201326592 | bytes 786432 | tf_op jit(solution)/shard_map/dot_general | solution.py:51
  35.0 0.7 copy-done.2
  35.7 2.0 %fusion.56 = f32[256,256]{1,0:T(8,128)} fusion(f32[256,256]{1,0:T(8,128)S(1)} %fusion.59, f32[1024,256]{1,0:T(8,128)} %all-gather.7.cloned.1.call-done), kind=kOutput, calls=%fused_computation.84 | convolution fusion | flops 201326592 | bytes 786432 | tf_op jit(solution)/shard_map/dot_general | solution.py:51
  37.7 0.7 fusion.55
  38.4 0.6 dynamic-slice
  39.2 1.0 copy.13
  42.1 5.4 %all-gather.2 = f32[128,256]{1,0:T(8,128)S(1)} all-gather(f32[32,256]{1,0:T(8,128)S(1)} %fusion.32), channel_id=4, replica_groups=mesh['line'=8,'span'=4] {'span'}, dimensions={0}, use_global_device_ids=true | all-gather | bytes 163840 | tf_op jit(solution)/shard_map/all_gather | solution.py:78
  48.3 33.9 %all-gather.3 = f32[256,256]{1,0:T(8,128)} all-gather(f32[32,256]{1,0:T(8,128)S(1)} %convolution_add_fusion.1), channel_id=5, replica_groups=mesh['line'=8,'span'=4] {'line'}, dimensions={0}, use_global_device_ids=true | all-gather | bytes 294912 | tf_op jit(solution)/shard_map/all_gather | solution.py:9
  82.2 0.7 slice_bitcast_fusion.16
  82.9 6.0 %all-gather.9.cloned.1.call-done = f32[2048,256]{1,0:T(8,128)} async-done(((f32[256,256]{1,0:T(8,128)}), f32[2048,256]{1,0:T(8,128)}) %all-gather.9.cloned.1.call-update) | async-done | bytes 2097168 | tf_op jit(solution)/shard_map/all_gather | solution.py:9
  88.9 8.8 %while.14 = (s32[]{:T(128)}, f32[32,256]{1,0:T(8,128)S(1)}, s32[]{:T(128)}, f32[8,256,256]{2,1,0:T(8,128)}, f32[8,32,256]{2,1,0:T(8,128)}, /*index=5*/s32[]{:T(128)}, s32[]{:T(128)}) while((s32[]{:T(128)}, f32[32,256]{1,0:T(8,128)S(1)}, s32[]{:T(128)}, f32[8,256,256]{2,1,0:T(8,128)}, f32[8,32,256]{2,1,0:T(8,128)}, ...), condition=%wide.region_1.2_spmd.clone, body=%wide.region_0.1_spmd.clone.sunk | while | flops 25198596 | bytes 461415 | solution.py:18
  88.9 1.2 %fusion.139 = f32[32,256]{1,0:T(8,128)S(1)} fusion(f32[8,256,256]{2,1,0:T(8,128)} %get-tuple-element.198, s32[]{:T(128)S(6)} %copy.16, f32[32,256]{1,0:T(8,128)S(1)} %copy.28, f32[8,32,256]{2,1,0:T(8,128)} %get-tuple-element.199, pred[]{:T(512)S(6)} %compare.3, pred[]{:T(512)S(6)} %lt.27), kind=kOutput, calls=%fused_computation.2.clone.1 | convolution fusion | flops 25198592 | bytes 395776 | tf_op jit(solution)/shard_map/while/body/eval_jaxpr/dot_general | solution.py:55
  90.2 1.2 %fusion.139 = f32[32,256]{1,0:T(8,128)S(1)} fusion(f32[8,256,256]{2,1,0:T(8,128)} %get-tuple-element.198, s32[]{:T(128)S(6)} %copy.16, f32[32,256]{1,0:T(8,128)S(1)} %copy.28, f32[8,32,256]{2,1,0:T(8,128)} %get-tuple-element.199, pred[]{:T(512)S(6)} %compare.3, pred[]{:T(512)S(6)} %lt.27), kind=kOutput, calls=%fused_computation.2.clone.1 | convolution fusion | flops 25198592 | bytes 395776 | tf_op jit(solution)/shard_map/while/body/eval_jaxpr/dot_general | solution.py:55
  91.5 1.2 %fusion.139 = f32[32,256]{1,0:T(8,128)S(1)} fusion(f32[8,256,256]{2,1,0:T(8,128)} %get-tuple-element.198, s32[]{:T(128)S(6)} %copy.16, f32[32,256]{1,0:T(8,128)S(1)} %copy.28, f32[8,32,256]{2,1,0:T(8,128)} %get-tuple-element.199, pred[]{:T(512)S(6)} %compare.3, pred[]{:T(512)S(6)} %lt.27), kind=kOutput, calls=%fused_computation.2.clone.1 | convolution fusion | flops 25198592 | bytes 395776 | tf_op jit(solution)/shard_map/while/body/eval_jaxpr/dot_general | solution.py:55
  92.7 1.2 %fusion.139 = f32[32,256]{1,0:T(8,128)S(1)} fusion(f32[8,256,256]{2,1,0:T(8,128)} %get-tuple-element.198, s32[]{:T(128)S(6)} %copy.16, f32[32,256]{1,0:T(8,128)S(1)} %copy.28, f32[8,32,256]{2,1,0:T(8,128)} %get-tuple-element.199, pred[]{:T(512)S(6)} %compare.3, pred[]{:T(512)S(6)} %lt.27), kind=kOutput, calls=%fused_computation.2.clone.1 | convolution fusion | flops 25198592 | bytes 395776 | tf_op jit(solution)/shard_map/while/body/eval_jaxpr/dot_general | solution.py:55
  94.0 1.2 %fusion.139 = f32[32,256]{1,0:T(8,128)S(1)} fusion(f32[8,256,256]{2,1,0:T(8,128)} %get-tuple-element.198, s32[]{:T(128)S(6)} %copy.16, f32[32,256]{1,0:T(8,128)S(1)} %copy.28, f32[8,32,256]{2,1,0:T(8,128)} %get-tuple-element.199, pred[]{:T(512)S(6)} %compare.3, pred[]{:T(512)S(6)} %lt.27), kind=kOutput, calls=%fused_computation.2.clone.1 | convolution fusion | flops 25198592 | bytes 395776 | tf_op jit(solution)/shard_map/while/body/eval_jaxpr/dot_general | solution.py:55
  95.2 1.2 %fusion.139 = f32[32,256]{1,0:T(8,128)S(1)} fusion(f32[8,256,256]{2,1,0:T(8,128)} %get-tuple-element.198, s32[]{:T(128)S(6)} %copy.16, f32[32,256]{1,0:T(8,128)S(1)} %copy.28, f32[8,32,256]{2,1,0:T(8,128)} %get-tuple-element.199, pred[]{:T(512)S(6)} %compare.3, pred[]{:T(512)S(6)} %lt.27), kind=kOutput, calls=%fused_computation.2.clone.1 | convolution fusion | flops 25198592 | bytes 395776 | tf_op jit(solution)/shard_map/while/body/eval_jaxpr/dot_general | solution.py:55
  96.5 1.2 %fusion.139 = f32[32,256]{1,0:T(8,128)S(1)} fusion(f32[8,256,256]{2,1,0:T(8,128)} %get-tuple-element.198, s32[]{:T(128)S(6)} %copy.16, f32[32,256]{1,0:T(8,128)S(1)} %copy.28, f32[8,32,256]{2,1,0:T(8,128)} %get-tuple-element.199, pred[]{:T(512)S(6)} %compare.3, pred[]{:T(512)S(6)} %lt.27), kind=kOutput, calls=%fused_computation.2.clone.1 | convolution fusion | flops 25198592 | bytes 395776 | tf_op jit(solution)/shard_map/while/body/eval_jaxpr/dot_general | solution.py:55
  97.7 1.9 %fusion.18 = f32[32,256]{1,0:T(8,128)S(1)} fusion(f32[32,256]{1,0:T(8,128)S(1)} %get-tuple-element.99, s32[]{:T(128)S(6)} %select_n.26, f32[1,256,256]{2,1,0:T(8,128)} %fusion.55, f32[1,256,256]{2,1,0:T(8,128)} %slice_bitcast_fusion.16, f32[1,256,256]{2,1,0:T(8,128)S(1)} %bitcast.236, f32[1,256,256]{2,1,0:T(8,128)} %bitcast.237, ...), kind=kOutput, calls=%fused_computation.31 | convolution fusion | flops 25411584 | bytes 1247236 | tf_op jit(solution)/shard_map/dot_general | solution.py:55
  101.8 8.4 %all_to_all.36 = f32[32,8,256]{2,1,0:T(8,128)S(1)} all-to-all(f32[32,8,256]{2,1,0:T(8,128)S(1)} %copy.8), channel_id=1, replica_groups=mesh['line'=8,'span'=4] {'span'}, dimensions={0} | all-to-all | bytes 524288 | tf_op jit(solution)/shard_map/all_to_all | solution.py:93
  110.2 0.7 copy.12
  (68 shorter events, 5.5 us)
Async XLA Ops:
  6.5 25.7 %all-gather.7.cloned.1.call-start = ((), (), s32[]{:S(2)}) async-start(), calls=%async_computation.2 | async-start | bytes 1310720 | tf_op jit(solution)/shard_map/all_gather | solution.py:77
  9.9 2.7 %copy-start.5 = (f32[8,32,256]{2,1,0:T(8,128)S(1)}, f32[8,32,256]{2,1,0:T(8,128)}, u32[]{:S(2)}) copy-start(f32[8,32,256]{2,1,0:T(8,128)} %param.5) | copy-start | bytes 786436
  12.6 26.5 %copy-start.6 = (f32[8,256]{1,0:T(8,128)S(1)}, f32[8,256]{1,0:T(8,128)}, u32[]{:S(2)}) copy-start(f32[8,256]{1,0:T(8,128)} %param.7) | copy-start | bytes 24580
  13.5 26.7 %copy-start = (f32[8,256,256]{2,1,0:T(8,128)S(1)}, f32[8,256,256]{2,1,0:T(8,128)}, u32[]{:S(2)}) copy-start(f32[8,256,256]{2,1,0:T(8,128)} %param.6) | copy-start | bytes 6291460
  13.5 25.7 %all-to-all-start = ((f32[8,32,256]{2,0,1:T(8,128)}), f32[8,32,256]{2,0,1:T(8,128)}, u32[]{:S(2)}, u32[]{:S(2)}) async-start(f32[8,32,256]{2,0,1:T(8,128)} %copy.6), calls=%async_computation | async-start | bytes 524288 | tf_op jit(solution)/shard_map/all_to_all | solution.py:69
  17.9 71.1 %all-gather.9.cloned.1.call-start = ((), (), s32[]{:S(2)}) async-start(), calls=%async_computation.3 | async-start | bytes 2359296 | tf_op jit(solution)/shard_map/all_gather | solution.py:9
  35.0 0.7 copy-start.2
  37.7 9.9 %copy-start.1 = (f32[1024,256]{1,0:T(8,128)S(1)}, f32[1024,256]{1,0:T(8,128)}, u32[]{:S(2)}) copy-start(f32[1024,256]{1,0:T(8,128)} %all-gather.7.cloned.1.call-done) | copy-start | bytes 3145732
  39.1 8.4 %copy-start.7 = (f32[1,256]{1,0:T(1,128)}, f32[1,256]{1,0:T(1,128)S(1)}, u32[]{:S(2)}) copy-start(f32[1,256]{1,0:T(1,128)S(1)} %get-tuple-element.129) | copy-start | bytes 3076
  39.1 8.4 %copy-start.9 = (f32[1,256]{1,0:T(1,128)}, f32[1,256]{1,0:T(1,128)S(1)}, u32[]{:S(2)}) copy-start(f32[1,256]{1,0:T(1,128)S(1)} %get-tuple-element.135) | copy-start | bytes 3076
  39.1 8.4 %copy-start.11 = (f32[1,256]{1,0:T(1,128)}, f32[1,256]{1,0:T(1,128)S(1)}, u32[]{:S(2)}) copy-start(f32[1,256]{1,0:T(1,128)S(1)} %get-tuple-element.134) | copy-start | bytes 3076
  39.1 8.4 %copy-start.13 = (f32[1,256]{1,0:T(1,128)}, f32[1,256]{1,0:T(1,128)S(1)}, u32[]{:S(2)}) copy-start(f32[1,256]{1,0:T(1,128)S(1)} %get-tuple-element.133) | copy-start | bytes 3076
  40.1 42.0 %copy-start.3 = (f32[8,4,8,256]{3,0,1,2:T(8,128)}, f32[8,4,8,256]{3,0,1,2:T(8,128)S(1)}, u32[]{:S(2)}) copy-start(f32[8,4,8,256]{3,0,1,2:T(8,128)S(1)} %copy.13) | copy-start | bytes 786436
  82.9 14.8 %copy-start.4 = (f32[8,4,8,256]{3,0,1,2:T(8,128)S(1)}, f32[8,4,8,256]{3,0,1,2:T(8,128)}, u32[]{:S(2)}) copy-start(f32[8,4,8,256]{3,0,1,2:T(8,128)} %copy-done.3) | copy-start | bytes 786436
  82.9 14.8 %copy-start.14 = (f32[1,256]{1,0:T(1,128)S(1)}, f32[1,256]{1,0:T(1,128)}, u32[]{:S(2)}) copy-start(f32[1,256]{1,0:T(1,128)} %copy-done.13) | copy-start | bytes 3076
  82.9 17.0 %copy-start.12 = (f32[1,256]{1,0:T(1,128)S(1)}, f32[1,256]{1,0:T(1,128)}, u32[]{:S(2)}) copy-start(f32[1,256]{1,0:T(1,128)} %copy-done.11) | copy-start | bytes 3076
  88.9 11.2 %copy-start.10 = (f32[1,256]{1,0:T(1,128)S(1)}, f32[1,256]{1,0:T(1,128)}, u32[]{:S(2)}) copy-start(f32[1,256]{1,0:T(1,128)} %copy-done.9) | copy-start | bytes 3076
  88.9 11.4 %copy-start.8 = (f32[1,256]{1,0:T(1,128)S(1)}, f32[1,256]{1,0:T(1,128)}, u32[]{:S(2)}) copy-start(f32[1,256]{1,0:T(1,128)} %copy-done.7) | copy-start | bytes 3076
Sparse Core Ops, SparseCore 0:
  12.7 19.4 all-gather.6
  37.8 51.0 all-gather.8
where the time goes:
time: 118 us
  blocking collectives  47.7 us (40%)
  matrix products  23 us (19%)
  waiting for transfers between devices  20.4 us (17%)
  between operations  13.8 us (12%)
  local copies, waits for them, and re-layouts  4.85 us (4%)
  starting transfers between devices  4.4 us (4%)
  other arithmetic  3.35 us (3%)
    all_gather x1, blocking collectives, carried_in(): pieces = jax.tree.map(lambda part: lax.all_gather(part, axis), value)  33.9 us
    all_gather x1, waiting for transfers between devices, shards(): lax.all_gather(spike_map[None], 'span', axis=0, tiled=True)  14.3 us
    dot_general x11, matrix products, combine(): jnp.dot(early_state, late_map, precision=lax.Precision.HIGHEST, preferred...  11.1 us
    all_to_all x1, blocking collectives, shards(): lax.all_to_all(solved, 'span', split_axis=0, concat_axis=1, tiled=True)  8.39 us
    all_gather x1, waiting for transfers between devices, carried_in(): pieces = jax.tree.map(lambda part: lax.all_gather(part, axis), value)  6.02 us
    all_gather x1, blocking collectives, shards(): lax.all_gather(last_states[None], 'span', axis=0, tiled=True)  5.42 us
    dot_general x3, matrix products, combine(): jnp.dot(early_map, late_map, precision=lax.Precision.HIGHEST, preferred_e...  4.77 us
    all_to_all x1, starting transfers between devices, shards(): lax.all_to_all(forcing, 'span', split_axis=1, concat_axis=0, tiled=True)  4.39 us
  transfers between devices with their start and end apart: 3, of which 2 were waited for; matrix products, arithmetic and copies ran while one was open for 10% of the time, Pallas kernels for 0%

commit v1 on v0

v1 whole, which is shorter than its diff:
```python
import functools

import jax
import jax.numpy as jnp
from jax import lax
from jax.experimental import pallas as pl
from jax.experimental.pallas import tpu as pltpu
from jax.sharding import PartitionSpec as P

MESH = pl.DeviceIdType.MESH
RUN = 2


def split(value):
    high = value.astype(jnp.bfloat16)
    return high, (value - high.astype(jnp.float32)).astype(jnp.bfloat16)


def dot(a, b):
    return jnp.dot(a, b, preferred_element_type=jnp.float32)


def times(value, high, low):
    rows = value.shape[0]
    value_high, value_low = split(value)
    both = dot(jnp.concatenate([value_high, value_low], axis=0), high)
    return both[:rows] + both[rows:] + dot(value_high, low)


def kernel(
    lines_count,
    span_count,
    forcing,
    blocks,
    upstream,
    out,
    cells_in,
    held,
    block_high,
    block_low,
    map_high,
    map_low,
    trial,
    pair_maps,
    pair_states,
    maps,
    states,
    ahead_maps,
    ahead_states,
    entering,
    leaving,
    solved,
    block_sem,
    force_send,
    force_recv,
    pair_send,
    pair_recv,
    map_send,
    map_recv,
    pass_send,
    pass_recv,
    state_send,
    state_recv,
    chain_send,
    chain_recv,
    out_sem,
    out_send,
    out_recv,
):
    line, span = lax.axis_index("line"), lax.axis_index("span")
    cells, levels = upstream.shape
    own_lines = forcing.shape[0]
    half_span = span_count // 2
    pairs = RUN * half_span
    runs = lines_count // RUN
    run, place = line // RUN, line % RUN
    row, core = span // 2, span % 2
    pair = place * half_span + row
    partner = (line, row * 2 + (1 - core))
    half = levels // 2
    mine = pl.ds(pl.multiple_of(core * half, half), half)

    shifts = [(a, b) for a in range(RUN) for b in range(half_span) if (a, b) != (0, 0)]

    def peer(shift, sign):
        other_place = (place + sign * shift[0] + RUN) % RUN
        other_row = (row + sign * shift[1] + half_span) % half_span
        return (run * RUN + other_place, other_row * 2 + core), other_place * half_span + other_row

    def remote(source, target, send, recv, device):
        return pltpu.make_async_remote_copy(
            src_ref=source,
            dst_ref=target,
            send_sem=send,
            recv_sem=recv,
            device_id=device,
            device_id_type=MESH,
        )

    loads = [
        pltpu.make_async_copy(blocks.at[cell], held.at[cell], block_sem.at[cell])
        for cell in range(cells)
    ]
    for load in loads:
        load.start()

    barrier = pltpu.get_barrier_semaphore()
    greeted = 0
    for step in range(1, span_count):
        pl.semaphore_signal(
            barrier, inc=1, device_id=(line, (span + step) % span_count), device_id_type=MESH
        )
        greeted += 1
    for shift in shifts:
        if shift[0] != 0:
            pl.semaphore_signal(barrier, inc=1, device_id=peer(shift, 1)[0], device_id_type=MESH)
            greeted += 1
    first, last = run == 0, run == runs - 1

    @pl.when(jnp.logical_not(first))
    def _():
        pl.semaphore_signal(barrier, inc=1, device_id=(line - RUN, span), device_id_type=MESH)

    @pl.when(jnp.logical_not(last))
    def _():
        pl.semaphore_signal(barrier, inc=1, device_id=(line + RUN, span), device_id_type=MESH)

    chained = jnp.where(first, 0, 1) + jnp.where(last, 0, 1)
    pl.semaphore_wait(barrier, greeted + chained)

    own_rows = pl.ds(pl.multiple_of(span * own_lines, own_lines), own_lines)
    own_cells = pl.ds(pl.multiple_of(span * cells, cells), cells)
    force_copies = []
    for step in range(1, span_count):
        other = (span + step) % span_count
        other_cells = pl.ds(pl.multiple_of(other * cells, cells), cells)
        copy = remote(
            forcing.at[:, other_cells, :],
            cells_in.at[own_rows],
            force_send.at[step],
            force_recv.at[step],
            (line, other),
        )
        copy.start()
        force_copies.append(copy)
    cells_in[own_rows] = forcing[:, own_cells, :]

    factors = -upstream[...]
    for cell in range(cells):
        loads[cell].wait()
        value = held[cell]
        high, low = split(value)
        block_high[cell] = high
        block_low[cell] = low
        if cell == 0:
            running = jnp.transpose(factors)[:, 0:1] * value
        else:
            running = times(running * factors[cell : cell + 1, :], high, low)
        if cell == cells - 1:
            pair_maps[core] = running
            map_copy = remote(
                pair_maps.at[core],
                pair_maps.at[core],
                pair_send.at[0],
                pair_recv.at[0],
                partner,
            )
            map_copy.start()
        high, low = split(running)
        map_high[cell] = high
        map_low[cell] = low

    map_copy.wait()
    late_high, late_low = split(pair_maps[1])
    maps[pair] = times(pair_maps[0], late_high, late_low)
    map_copies = []
    for index, shift in enumerate(shifts):
        copy = remote(
            maps.at[pair, mine],
            maps.at[pair, mine],
            map_send.at[index],
            map_recv.at[index],
            peer(shift, 1)[0],
        )
        copy.start()
        map_copies.append(copy)

    for copy in force_copies:
        copy.wait()
    by_cell = jnp.transpose(cells_in[...], (1, 0, 2))
    for cell in range(cells):
        right = by_cell[cell]
        if cell > 0:
            right = right + factors[cell : cell + 1, :] * carried
        carried = times(right, block_high[cell], block_low[cell])
        trial[cell] = carried
    pair_states[core] = carried
    state_copy = remote(
        pair_states.at[core], pair_states.at[core], pair_send.at[1], pair_recv.at[1], partner
    )
    state_copy.start()
    state_copy.wait()
    states[pair] = times(pair_states[0], late_high, late_low) + pair_states[1]
    state_copies = []
    for index, shift in enumerate(shifts):
        copy = remote(
            states.at[pair],
            states.at[pair],
            state_send.at[index],
            state_recv.at[index],
            peer(shift, 1)[0],
        )
        copy.start()
        state_copies.append(copy)

    passed = []
    for index, shift in enumerate(shifts):
        map_copies[index].wait_recv()
        sender = peer(shift, -1)[1]
        copy = remote(
            maps.at[sender, mine],
            maps.at[sender, mine],
            pass_send.at[index],
            pass_recv.at[index],
            partner,
        )
        copy.start()
        passed.append(copy)
    for copy in passed:
        copy.wait_recv()
    for copy in state_copies:
        copy.wait_recv()

    shape = (levels, levels)
    eye = lax.broadcasted_iota(jnp.int32, shape, 0) == lax.broadcasted_iota(jnp.int32, shape, 1)
    ahead_maps[0] = jnp.where(eye, 1.0, 0.0).astype(jnp.float32)
    ahead_states[0] = jnp.zeros(ahead_states.shape[1:], jnp.float32)
    joined_map, joined_state = maps[0], states[0]
    for index in range(1, pairs):
        ahead_maps[index] = joined_map
        ahead_states[index] = joined_state
        high, low = split(maps[index])
        joined = times(jnp.concatenate([joined_map, joined_state], axis=0), high, low)
        joined_map = joined[:levels]
        joined_state = joined[levels:] + states[index]

    chain = remote(
        leaving, entering, chain_send.at[0], chain_recv.at[0], ((line + RUN) % lines_count, span)
    )

    @pl.when(first)
    def _():
        leaving[...] = joined_state
        entering[...] = jnp.zeros(entering.shape, jnp.float32)
        chain.start()

    joined_high, joined_low = split(joined_map)

    early_high, early_low = split(pair_maps[0])
    before = jnp.concatenate([ahead_maps[pair], ahead_states[pair]], axis=0)
    after = times(before, early_high, early_low)
    own_map = jnp.where(core == 1, after[:levels], before[:levels])
    own_state = jnp.where(core == 1, after[levels:] + pair_states[0], before[levels:])
    own_high, own_low = split(own_map)

    @pl.when(jnp.logical_not(first))
    def _():
        chain.wait_recv()
        leaving[...] = times(entering[...], joined_high, joined_low) + joined_state

        @pl.when(jnp.logical_not(last))
        def _():
            chain.start()

    incoming = times(entering[...], own_high, own_low) + own_state
    pieces = [
        trial[cell] + times(incoming, map_high[cell], map_low[cell]) for cell in range(cells)
    ]
    solved[...] = jnp.transpose(jnp.stack(pieces, axis=0), (1, 0, 2))

    out_copies = []
    for step in range(1, span_count):
        other = (span + step) % span_count
        other_rows = pl.ds(pl.multiple_of(other * own_lines, own_lines), own_lines)
        copy = remote(
            solved.at[other_rows],
            out.at[:, own_cells, :],
            out_send.at[step],
            out_recv.at[step],
            (line, other),
        )
        copy.start()
        out_copies.append(copy)
    keep = pltpu.make_async_copy(solved.at[own_rows], out.at[:, own_cells, :], out_sem)
    keep.start()
    for copy in map_copies + passed + state_copies:
        copy.wait_send()

    @pl.when(jnp.logical_not(last))
    def _():
        chain.wait_send()

    keep.wait()
    for copy in out_copies:
        copy.wait()


def shards(lines_count, span_count, forcing, blocks, upstream):
    own_lines, _, levels = forcing.shape
    cells = blocks.shape[0]
    lines = own_lines * span_count
    pairs = RUN * (span_count // 2)
    f32, bf16 = jnp.float32, jnp.bfloat16
    dma = pltpu.SemaphoreType.DMA
    return pl.pallas_call(
        functools.partial(kernel, lines_count, span_count),
        out_shape=jax.ShapeDtypeStruct(forcing.shape, f32),
        in_specs=[
            pl.BlockSpec(memory_space=pltpu.VMEM),
            pl.BlockSpec(memory_space=pl.ANY),
            pl.BlockSpec(memory_space=pltpu.VMEM),
        ],
        out_specs=pl.BlockSpec(memory_space=pl.ANY),
        scratch_shapes=[
            pltpu.VMEM((lines, cells, levels), f32),
            pltpu.VMEM((cells, levels, levels), f32),
            pltpu.VMEM((cells, levels, levels), bf16),
            pltpu.VMEM((cells, levels, levels), bf16),
            pltpu.VMEM((cells, levels, levels), bf16),
            pltpu.VMEM((cells, levels, levels), bf16),
            pltpu.VMEM((cells, lines, levels), f32),
            pltpu.VMEM((2, levels, levels), f32),
            pltpu.VMEM((2, lines, levels), f32),
            pltpu.VMEM((pairs, levels, levels), f32),
            pltpu.VMEM((pairs, lines, levels), f32),
            pltpu.VMEM((pairs, levels, levels), f32),
            pltpu.VMEM((pairs, lines, levels), f32),
            pltpu.VMEM((lines, levels), f32),
            pltpu.VMEM((lines, levels), f32),
            pltpu.VMEM((lines, cells, levels), f32),
            dma((cells,)),
            dma((span_count,)),
            dma((span_count,)),
            dma((2,)),
            dma((2,)),
            dma((pairs,)),
            dma((pairs,)),
            dma((pairs,)),
            dma((pairs,)),
            dma((pairs,)),
            dma((pairs,)),
            dma((1,)),
            dma((1,)),
            dma,
            dma((span_count,)),
            dma((span_count,)),
        ],
        compiler_params=pltpu.CompilerParams(
            collective_id=0, has_side_effects=True, vmem_limit_bytes=48 << 20
        ),
    )(forcing, blocks, upstream)


def solution(mesh):
    placed = (P("span", "line", None), P(("line", "span"), None, None), P(("line", "span"), None))
    return jax.shard_map(
        functools.partial(shards, mesh.shape["line"], mesh.shape["span"]),
        mesh=mesh,
        in_specs=placed,
        out_specs=P("span", "line", None),
        check_vma=False,
    )
```

time: 118 us -> 34 us (0.29)
  the two profiles are of different devices: /device:TPU:0 before, /device:TPU:25 now
where the time goes in v1:
time: 34 us; the launch traced here: 33.8 us
  Pallas kernels  29.9 us (88%)
  local copies, waits for them, and re-layouts  3.94 us (12%)
    pallas_call x1, Pallas kernels, shards(): pl.pallas_call(functools.partial(kernel, lines_count, span_count), out_sh...  29.9 us
    unnamed x7, local copies, waits for them, and re-layouts  3.94 us

profile of v1, /device:TPU:25, one launch (start us, length us, event | category | flops | bytes accessed | tf_op | source)
XLA Modules:
  0.0 33.8 jit_solution(12698728912684900872)
XLA Ops:
  0.0 0.0 copy-start
  0.0 1.6 %copy-done = f32[8,256,256]{2,1,0:T(8,128)S(1)} copy-done((f32[8,256,256]{2,1,0:T(8,128)S(1)}, f32[8,256,256]{2,1,0:T(8,128)}, u32[]{:S(2)}) %copy-start) | copy-done | bytes 2097176
  1.6 0.0 copy-start.1
  1.6 0.9 %copy-done.1 = f32[8,32,256]{2,1,0:T(8,128)S(1)} copy-done((f32[8,32,256]{2,1,0:T(8,128)S(1)}, f32[8,32,256]{2,1,0:T(8,128)}, u32[]{:S(2)}) %copy-start.1) | copy-done | bytes 262168
  2.5 0.0 copy-start.2
  2.5 0.7 %copy-done.2 = f32[8,256]{1,0:T(8,128)S(1)} copy-done((f32[8,256]{1,0:T(8,128)S(1)}, f32[8,256]{1,0:T(8,128)}, u32[]{:S(2)}) %copy-start.2) | copy-done | bytes 8216
  3.2 29.9 %shard_map.37 = f32[8,32,256]{2,1,0:T(8,128)S(1)} custom-call(f32[8,32,256]{2,1,0:T(8,128)S(1)} %copy-done.1, f32[8,256,256]{2,1,0:T(8,128)S(1)} %copy-done, f32[8,256]{1,0:T(8,128)S(1)} %copy-done.2), custom_call_target="tpu_custom_call" | custom-call | tf_op jit(solution)/shard_map/pallas_call | solution.py:315
  33.1 0.7 %copy.5 = f32[8,32,256]{2,1,0:T(8,128)} copy(f32[8,32,256]{2,1,0:T(8,128)S(1)} %shard_map.37) | data formatting | bytes 524288
Async XLA Ops:
  0.0 1.6 %copy-start = (f32[8,256,256]{2,1,0:T(8,128)S(1)}, f32[8,256,256]{2,1,0:T(8,128)}, u32[]{:S(2)}) copy-start(f32[8,256,256]{2,1,0:T(8,128)} %blocks.1) | copy-start | bytes 6291460
  1.6 0.9 %copy-start.1 = (f32[8,32,256]{2,1,0:T(8,128)S(1)}, f32[8,32,256]{2,1,0:T(8,128)}, u32[]{:S(2)}) copy-start(f32[8,32,256]{2,1,0:T(8,128)} %forcing.1) | copy-start | bytes 786436
  2.5 0.7 %copy-start.2 = (f32[8,256]{1,0:T(8,128)S(1)}, f32[8,256]{1,0:T(8,128)}, u32[]{:S(2)}) copy-start(f32[8,256]{1,0:T(8,128)} %upstream.1) | copy-start | bytes 24580

commit v2 on v1

--- a/solution.py
+++ b/solution.py
@@ -50,6 +50,11 @@
     entering,
     leaving,
     solved,
+    factors_in,
+    right_high,
+    right_low,
+    factor_sem,
+    force_sem,
     block_sem,
     force_send,
     force_recv,
@@ -101,6 +106,8 @@
         pltpu.make_async_copy(blocks.at[cell], held.at[cell], block_sem.at[cell])
         for cell in range(cells)
     ]
+    factor_load = pltpu.make_async_copy(upstream, factors_in, factor_sem)
+    factor_load.start()
     for load in loads:
         load.start()
 
@@ -126,26 +133,15 @@
         pl.semaphore_signal(barrier, inc=1, device_id=(line + RUN, span), device_id_type=MESH)
 
     chained = jnp.where(first, 0, 1) + jnp.where(last, 0, 1)
-    pl.semaphore_wait(barrier, greeted + chained)
 
     own_rows = pl.ds(pl.multiple_of(span * own_lines, own_lines), own_lines)
     own_cells = pl.ds(pl.multiple_of(span * cells, cells), cells)
+    stay = pltpu.make_async_copy(forcing.at[:, own_cells, :], cells_in.at[own_rows], force_sem)
+    stay.start()
+
     force_copies = []
-    for step in range(1, span_count):
-        other = (span + step) % span_count
-        other_cells = pl.ds(pl.multiple_of(other * cells, cells), cells)
-        copy = remote(
-            forcing.at[:, other_cells, :],
-            cells_in.at[own_rows],
-            force_send.at[step],
-            force_recv.at[step],
-            (line, other),
-        )
-        copy.start()
-        force_copies.append(copy)
-    cells_in[own_rows] = forcing[:, own_cells, :]
-
-    factors = -upstream[...]
+    factor_load.wait()
+    factors = -factors_in[...]
     for cell in range(cells):
         loads[cell].wait()
         value = held[cell]
@@ -169,6 +165,20 @@
         high, low = split(running)
         map_high[cell] = high
         map_low[cell] = low
+        if cell == min(2, cells - 2):
+            pl.semaphore_wait(barrier, greeted + chained)
+            for step in range(1, span_count):
+                other = (span + step) % span_count
+                other_cells = pl.ds(pl.multiple_of(other * cells, cells), cells)
+                copy = remote(
+                    forcing.at[:, other_cells, :],
+                    cells_in.at[own_rows],
+                    force_send.at[step],
+                    force_recv.at[step],
+                    (line, other),
+                )
+                copy.start()
+                force_copies.append(copy)
 
     map_copy.wait()
     late_high, late_low = split(pair_maps[1])
@@ -185,6 +195,7 @@
         copy.start()
         map_copies.append(copy)
 
+    stay.wait()
     for copy in force_copies:
         copy.wait()
     by_cell = jnp.transpose(cells_in[...], (1, 0, 2))
@@ -235,14 +246,13 @@
     eye = lax.broadcasted_iota(jnp.int32, shape, 0) == lax.broadcasted_iota(jnp.int32, shape, 1)
     ahead_maps[0] = jnp.where(eye, 1.0, 0.0).astype(jnp.float32)
     ahead_states[0] = jnp.zeros(ahead_states.shape[1:], jnp.float32)
-    joined_map, joined_state = maps[0], states[0]
+    joined_state = states[0]
     for index in range(1, pairs):
-        ahead_maps[index] = joined_map
         ahead_states[index] = joined_state
         high, low = split(maps[index])
-        joined = times(jnp.concatenate([joined_map, joined_state], axis=0), high, low)
-        joined_map = joined[:levels]
-        joined_state = joined[levels:] + states[index]
+        right_high[index] = high
+        right_low[index] = low
+        joined_state = times(joined_state, high, low) + states[index]
 
     chain = remote(
         leaving, entering, chain_send.at[0], chain_recv.at[0], ((line + RUN) % lines_count, span)
@@ -254,6 +264,10 @@
         entering[...] = jnp.zeros(entering.shape, jnp.float32)
         chain.start()
 
+    joined_map = maps[0]
+    for index in range(1, pairs):
+        ahead_maps[index] = joined_map
+        joined_map = times(joined_map, right_high[index], right_low[index])
     joined_high, joined_low = split(joined_map)
 
     early_high, early_low = split(pair_maps[0])
@@ -316,9 +330,9 @@
         functools.partial(kernel, lines_count, span_count),
         out_shape=jax.ShapeDtypeStruct(forcing.shape, f32),
         in_specs=[
-            pl.BlockSpec(memory_space=pltpu.VMEM),
             pl.BlockSpec(memory_space=pl.ANY),
-            pl.BlockSpec(memory_space=pltpu.VMEM),
+            pl.BlockSpec(memory_space=pl.ANY),
+            pl.BlockSpec(memory_space=pl.ANY),
         ],
         out_specs=pl.BlockSpec(memory_space=pl.ANY),
         scratch_shapes=[
@@ -338,6 +352,11 @@
             pltpu.VMEM((lines, levels), f32),
             pltpu.VMEM((lines, levels), f32),
             pltpu.VMEM((lines, cells, levels), f32),
+            pltpu.VMEM((cells, levels), f32),
+            pltpu.VMEM((pairs, levels, levels), bf16),
+            pltpu.VMEM((pairs, levels, levels), bf16),
+            dma,
+            dma,
             dma((cells,)),
             dma((span_count,)),
             dma((span_count,)),
@@ -356,7 +375,7 @@
             dma((span_count,)),
         ],
         compiler_params=pltpu.CompilerParams(
-            collective_id=0, has_side_effects=True, vmem_limit_bytes=48 << 20
+            collective_id=0, has_side_effects=True, vmem_limit_bytes=67043328
         ),
     )(forcing, blocks, upstream)
 

time: 34 us -> 30.9 us (0.909)
  local copies, waits for them, and re-layouts: 3.94 us -> 1.67 us
  Pallas kernels: 29.9 us -> 29 us
    unnamed x7 -> x1, local copies, waits for them, and re-layouts: 3.94 us -> 1.67 us
    pallas_call x1, Pallas kernels: 29.9 us -> 29 us  [shards(): pl.pallas_call(functools.partial(kernel, lines_count, span_count), out_sh...]
where the time goes in v2:
time: 30.9 us; the launch traced here: 30.7 us
  Pallas kernels  29 us (94%)
  local copies, waits for them, and re-layouts  1.67 us (5%)
    pallas_call x1, Pallas kernels, shards(): pl.pallas_call(functools.partial(kernel, lines_count, span_count), out_sh...  29 us
    unnamed x1, local copies, waits for them, and re-layouts  1.67 us

profile of v2, /device:TPU:25, one launch (start us, length us, event | category | flops | bytes accessed | tf_op | source)
XLA Modules:
  0.0 30.7 jit_solution(2208395480563768806)
XLA Ops:
  0.0 29.0 %shard_map.37 = f32[8,32,256]{2,1,0:T(8,128)} custom-call(f32[8,32,256]{2,1,0:T(8,128)} %forcing.1, f32[8,256,256]{2,1,0:T(8,128)} %blocks.1, f32[8,256]{1,0:T(8,128)} %upstream.1), custom_call_target="tpu_custom_call" | custom-call | tf_op jit(solution)/shard_map/pallas_call | solution.py:329
  29.0 1.7 %copy.5 = f32[8,32,256]{2,1,0:T(8,128)} copy(f32[8,32,256]{2,1,0:T(8,128)} %shard_map.37) | data formatting | bytes 524288

commit v3 on v2

--- a/solution.py
+++ b/solution.py
@@ -375,9 +375,9 @@
             dma((span_count,)),
         ],
         compiler_params=pltpu.CompilerParams(
-            collective_id=0, has_side_effects=True, vmem_limit_bytes=67043328
+            collective_id=0, has_side_effects=True, vmem_limit_bytes=48 << 20
         ),
-    )(forcing, blocks, upstream)
+    )(*[pltpu.with_memory_space_constraint(x, pltpu.MemorySpace.HBM) for x in (forcing, blocks, upstream)])
 
 
 def solution(mesh):

time: 30.9 us -> 29.8 us (0.964)
  local copies, waits for them, and re-layouts: 1.67 us -> 0.71 us
    unnamed x1, local copies, waits for them, and re-layouts: 1.67 us -> 0.71 us
where the time goes in v3:
time: 29.8 us; the launch traced here: 29.6 us
  Pallas kernels  28.9 us (97%)
  local copies, waits for them, and re-layouts  0.71 us (2%)
    pallas_call x1, Pallas kernels, shards(): pl.pallas_call(functools.partial(kernel, lines_count, span_count), out_sh...  28.9 us
    unnamed x1, local copies, waits for them, and re-layouts  0.71 us

profile of v3, /device:TPU:25, one launch (start us, length us, event | category | flops | bytes accessed | tf_op | source)
XLA Modules:
  0.0 29.6 jit_solution(5328839977078375613)
XLA Ops:
  0.0 28.9 %shard_map.37 = f32[8,32,256]{2,1,0:T(8,128)S(1)} custom-call(f32[8,32,256]{2,1,0:T(8,128)} %forcing.1, f32[8,256,256]{2,1,0:T(8,128)} %blocks.1, f32[8,256]{1,0:T(8,128)} %upstream.1), custom_call_target="tpu_custom_call" | custom-call | tf_op jit(solution)/shard_map/pallas_call | solution.py:329
  28.9 0.7 %copy.5 = f32[8,32,256]{2,1,0:T(8,128)} copy(f32[8,32,256]{2,1,0:T(8,128)S(1)} %shard_map.37) | data formatting | bytes 524288

commit v4 on v3

--- a/solution.py
+++ b/solution.py
@@ -86,6 +86,7 @@
     mine = pl.ds(pl.multiple_of(core * half, half), half)
 
     shifts = [(a, b) for a in range(RUN) for b in range(half_span) if (a, b) != (0, 0)]
+    shifts.sort(key=lambda shift: (shift[0] == 0) + (shift[1] == 0))
 
     def peer(shift, sign):
         other_place = (place + sign * shift[0] + RUN) % RUN

time: 29.8 us -> 29.8 us (level)
  no operation moved by 1% of the time
where the time goes in v4:
time: 29.8 us; the launch traced here: 29.7 us
  Pallas kernels  29 us (97%)
  local copies, waits for them, and re-layouts  0.71 us (2%)
    pallas_call x1, Pallas kernels, shards(): pl.pallas_call(functools.partial(kernel, lines_count, span_count), out_sh...  29 us
    unnamed x1, local copies, waits for them, and re-layouts  0.71 us

profile of v4, /device:TPU:25, one launch (start us, length us, event | category | flops | bytes accessed | tf_op | source)
XLA Modules:
  0.0 29.7 jit_solution(13679364998269517199)
XLA Ops:
  0.0 29.0 %shard_map.37 = f32[8,32,256]{2,1,0:T(8,128)S(1)} custom-call(f32[8,32,256]{2,1,0:T(8,128)} %forcing.1, f32[8,256,256]{2,1,0:T(8,128)} %blocks.1, f32[8,256]{1,0:T(8,128)} %upstream.1), custom_call_target="tpu_custom_call" | custom-call | tf_op jit(solution)/shard_map/pallas_call | solution.py:330
  29.0 0.7 %copy.5 = f32[8,32,256]{2,1,0:T(8,128)} copy(f32[8,32,256]{2,1,0:T(8,128)S(1)} %shard_map.37) | data formatting | bytes 524288
